TPU v7x, 512 devices: a whole 4x8x8 slice. The times are simulated.
512 devices in a mesh: dp: 4 (over x), ep: 128 (over z, y, core).
Axes of the slice: x: 4, y: 8, z: 8, core: 2. Of those that a mesh axis runs over, the one named last changes fastest.
Arguments:
- tokens: bfloat16 [128, 16, 2048], P('ep', 'dp'), may hold values from -6 to 6
- dest_ids: int32 [128, 16, 8], P('ep', 'dp'), may hold values from 0 to 127, all different within a row; in each aligned block of 16 rows (0 to 15, 16 to 31, ..., all dimensions but the last counted through in order) at most 2 rows name the same one
- gate_fixed: int32 [128, 16, 8], P('ep', 'dp'), may hold values from 1 to 65535
- gate_up: bfloat16 [128, 2, 768, 2048], P('ep', None, 'dp'), may hold values from -0.125 to 0.125
- down: bfloat16 [128, 768, 2048], P('ep', 'dp'), may hold values from -0.21875 to 0.21875
Outputs:
- mixed: bfloat16 [128, 16, 2048], P('ep', 'dp')
Inputs may be any that keep to these rules, and one draw needn't show every extreme that they name: `dest_ids`: each row names 8 different experts; within one column's 16 rows no expert is named by more than 2 routes.
All inputs are finite; a program needn't handle non-finite values.
Results may differ from a plain program's by a relative error of at most 0.012.
Values may be sent and summed in bfloat16 or wider, within the bound.
A program may use at most 192 MiB of HBM per device.

v0:
```python
import jax
import jax.numpy as jnp
from jax import lax
from jax.sharding import PartitionSpec as P


def feed_forward(rows, pair, lower):
    gate = jnp.einsum("nd,hd->nh", rows, pair[0], preferred_element_type=jnp.float32)
    upper = jnp.einsum("nd,hd->nh", rows, pair[1], preferred_element_type=jnp.float32)
    hidden = (jax.nn.silu(gate) * upper).astype(jnp.bfloat16)
    return jnp.dot(hidden, lower, preferred_element_type=jnp.float32).astype(jnp.bfloat16)


def per_device(tokens, dest_ids, gate_fixed, gate_up, down):
    peer_count = lax.axis_size("ep")
    own_rows = tokens[0]
    width = own_rows.shape[1]
    top_count = dest_ids.shape[2]
    gates = gate_fixed[0]
    route_table = jnp.concatenate([dest_ids[0], gates >> 8, gates & 255], axis=1)
    route_pad = jnp.pad(route_table, ((0, 0), (0, 128 - 3 * top_count))).astype(jnp.bfloat16)
    packed = lax.all_gather(
        jnp.concatenate([own_rows, route_pad], axis=1), "dp", axis=0, tiled=True
    )
    column_rows = packed[:, :width]
    table = packed[:, width : width + 3 * top_count].astype(jnp.int32)
    column_table = jnp.concatenate(
        [
            table[:, :top_count],
            table[:, top_count : 2 * top_count] * 256 + table[:, 2 * top_count :],
        ],
        axis=1,
    )
    col_rows = column_table.shape[0]
    capacity = min(col_rows, max(2, 2 * col_rows * top_count // peer_count))
    target_dev = column_table[:, :top_count].reshape(-1)
    gate_raw = column_table[:, top_count:].astype(jnp.float32)
    gate_norm = gate_raw / jnp.sum(gate_raw, axis=1, keepdims=True)
    marks = (target_dev[:, None] == jnp.arange(peer_count, dtype=jnp.int32)[None, :]).astype(
        jnp.int32
    )
    slot_rank = jnp.sum(jnp.cumsum(marks, axis=0) * marks, axis=1) - 1
    slot_index = target_dev * capacity + slot_rank
    source_row = jnp.arange(target_dev.shape[0], dtype=jnp.int32) // top_count
    send_block = (
        jnp.zeros((peer_count * capacity, width), jnp.bfloat16)
        .at[slot_index]
        .set(column_rows[source_row])
        .reshape(peer_count, capacity, width)
    )
    rows = lax.all_to_all(send_block, "ep", split_axis=0, concat_axis=0, tiled=True)
    flat_rows = rows.reshape(-1, rows.shape[2])
    own_out = feed_forward(flat_rows, gate_up[0], down[0])
    returned = lax.all_to_all(
        own_out.reshape(rows.shape[0], rows.shape[1], -1),
        "ep",
        split_axis=0,
        concat_axis=0,
        tiled=True,
    )
    flat_back = returned.reshape(peer_count * capacity, -1)
    weighted = flat_back[slot_index].astype(jnp.float32) * gate_norm.reshape(-1)[:, None]
    summed = jnp.sum(weighted.reshape(col_rows, top_count, -1), axis=1)
    parts = lax.all_to_all(
        summed.astype(jnp.bfloat16).reshape(4, -1, width),
        "dp",
        split_axis=0,
        concat_axis=0,
        tiled=True,
    )
    mine = jnp.sum(parts.astype(jnp.float32), axis=0).astype(jnp.bfloat16)
    return mine[None]


def solution(mesh):
    return jax.shard_map(
        per_device,
        mesh=mesh,
        in_specs=(
            P("ep", "dp", None),
            P("ep", "dp", None),
            P("ep", "dp", None),
            P("ep", None, "dp", None),
            P("ep", "dp", None),
        ),
        out_specs=P("ep", "dp", None),
        check_vma=False,
    )
```

profile of v0, /device:TPU:8, one launch (start us, length us, event | category | flops | bytes accessed | tf_op | source)
XLA Modules:
  0.0 122.4 jit_solution(11102416586996701243)
XLA Ops:
  0.0 0.0 copy-start
  0.0 0.8 fusion.25
  0.8 0.1 fusion.28
  0.9 0.7 maximum_bitcast_fusion
  1.6 12.2 %all-gather = bf16[4,4,2176]{2,1,0:T(4,128)(2,1)S(1)} all-gather(bf16[1,4,2176]{2,1,0:T(4,128)(2,1)S(1)} %maximum_bitcast_fusion), channel_id=1, replica_groups=mesh['dp'=4,'ep'=128] {'dp'}, dimensions={0}, use_global_device_ids=true | all-gather | bytes 87040 | tf_op jit(solution)/shard_map/all_gather | solution.py:22
  13.9 0.1 eq.15
  14.0 0.1 fusion.19
  14.1 0.2 reduce_window_sum.11
  14.3 0.2 select_reduce_fusion
  14.4 0.1 mul.43
  14.5 3.4 %scatter_custom_fusion = bf16[256,2048]{1,0:T(8,128)(2,1)S(1)} fusion(s32[128]{0:T(128)S(1)} %fusion.30, bf16[16,2048]{1,0:T(8,128)(2,1)S(1)} %slice.36, s32[1024]{0:T(1024)S(1)} %pad_clamp_fusion.1, bf16[]{:T(256)} %constant.33.clone.1), kind=kCustom, calls=%fused_computation.14 | custom fusion | bytes 1048578 | tf_op jit(solution)/shard_map/scatter | solution.py:48
  17.9 0.7 reshape.114
  18.6 48.6 %all_to_all.15 = bf16[128,2,2048]{2,1,0:T(2,128)(2,1)S(1)} all-to-all(bf16[128,2,2048]{2,1,0:T(2,128)(2,1)S(1)} %reshape.114), channel_id=1, replica_groups=mesh['dp'=4,'ep'=128] {'ep'}, dimensions={0} | all-to-all | bytes 2097152 | tf_op jit(solution)/shard_map/all_to_all | solution.py:51
  67.2 0.4 reshape.115
  67.7 1.6 %fusion.5 = f32[256,192]{0,1:T(8,128)S(1)} fusion(bf16[256,2048]{1,0:T(8,128)(2,1)S(1)} %reshape.115, bf16[1,2,192,2048]{3,2,1,0:T(8,128)(2,1)} %param.8), kind=kOutput, calls=%fused_computation.10 | convolution fusion | flops 201326592 | bytes 2031616 | tf_op jit(solution)/shard_map/nd,hd->nh/dot_general | solution.py:8
  69.3 0.0 copy-done
  69.3 2.6 %convolution_convert_fusion = bf16[256,2048]{1,0:T(8,128)(2,1)S(1)} fusion(bf16[256,2048]{1,0:T(8,128)(2,1)S(1)} %reshape.115, bf16[1,192,2048]{2,1,0:T(8,128)(2,1)S(1)} %copy-done, bf16[1,2,192,2048]{3,2,1,0:T(8,128)(2,1)} %param.8, f32[256,192]{0,1:T(8,128)S(1)} %fusion.5), kind=kOutput, calls=%fused_computation.3 | convolution fusion | flops 403472384 | bytes 3866624 | tf_op jit(solution)/shard_map/dot_general | solution.py:11
  71.9 1.5 %reshape.116 = bf16[128,2,2048]{2,1,0:T(2,128)(2,1)} reshape(bf16[256,2048]{1,0:T(8,128)(2,1)S(1)} %convolution_convert_fusion) | data formatting | bytes 2097152 | tf_op jit(solution)/shard_map/reshape | solution.py:55
  73.4 5.9 %all-to-all-start.1 = ((bf16[128,2,2048]{2,1,0:T(2,128)(2,1)}), bf16[128,2,2048]{2,1,0:T(2,128)(2,1)S(1)}, u32[]{:S(2)}, u32[]{:S(2)}) async-start(bf16[128,2,2048]{2,1,0:T(2,128)(2,1)} %reshape.116), calls=%async_computation.1 | async-start | bytes 2097152 | tf_op jit(solution)/shard_map/all_to_all | solution.py:54
  79.4 0.2 fusion.21
  79.6 0.1 broadcast_divide_fusion
  79.6 31.2 %all-to-all-done.1 = bf16[128,2,2048]{2,1,0:T(2,128)(2,1)S(1)} async-done(((bf16[128,2,2048]{2,1,0:T(2,128)(2,1)}), bf16[128,2,2048]{2,1,0:T(2,128)(2,1)S(1)}, u32[]{:S(2)}, u32[]{:S(2)}) %all-to-all-start.1) | async-done | bytes 1048608 | tf_op jit(solution)/shard_map/all_to_all | solution.py:54
  110.8 0.4 reshape.117
  111.2 0.9 gather_fusion
  112.2 0.5 fusion.1
  112.7 9.1 %all_to_all.16 = bf16[4,4,2048]{2,1,0:T(4,128)(2,1)S(1)} all-to-all(bf16[4,4,2048]{2,1,0:T(4,128)(2,1)S(1)} %convert_element_type.40), channel_id=1, replica_groups=mesh['dp'=4,'ep'=128] {'dp'}, dimensions={0} | all-to-all | bytes 131072 | tf_op jit(solution)/shard_map/all_to_all | solution.py:64
  121.8 0.6 reduce_sum.42
  (9 shorter events, 0.1 us)
Async XLA Ops:
  0.0 69.3 %copy-start = (bf16[1,192,2048]{2,1,0:T(8,128)(2,1)S(1)}, bf16[1,192,2048]{2,1,0:T(8,128)(2,1)}, u32[]{:S(2)}) copy-start(bf16[1,192,2048]{2,1,0:T(8,128)(2,1)} %param.9) | copy-start | bytes 2359300
  73.4 37.4 %all-to-all-start.1 = ((bf16[128,2,2048]{2,1,0:T(2,128)(2,1)}), bf16[128,2,2048]{2,1,0:T(2,128)(2,1)S(1)}, u32[]{:S(2)}, u32[]{:S(2)}) async-start(bf16[128,2,2048]{2,1,0:T(2,128)(2,1)} %reshape.116), calls=%async_computation.1 | async-start | bytes 2097152 | tf_op jit(solution)/shard_map/all_to_all | solution.py:54
where the time goes:
time: 123 us; the launch traced here: 122 us
  blocking collectives  69.9 us (57%)
  waiting for transfers between devices  31.2 us (25%)
  local copies, waits for them, and re-layouts  7.6 us (6%)
  starting transfers between devices  5.94 us (5%)
  matrix products  4.2 us (3%)
  other arithmetic  3.41 us (3%)
    all_to_all x1, blocking collectives, per_device(): lax.all_to_all(send_block, 'ep', split_axis=0, concat_axis=0, tiled=True)  48.6 us
    all_to_all x1, waiting for transfers between devices, per_device(): lax.all_to_all(own_out.reshape(rows.shape[0], rows.shape[1], -1), 'ep', s...  31.2 us
    all_gather x1, blocking collectives, per_device(): lax.all_gather(jnp.concatenate([own_rows, route_pad], axis=1), 'dp', axis...  12.2 us
    all_to_all x1, blocking collectives, per_device(): lax.all_to_all(summed.astype(jnp.bfloat16).reshape(4, -1, width), 'dp', s...  9.09 us
    all_to_all x1, starting transfers between devices, per_device(): lax.all_to_all(own_out.reshape(rows.shape[0], rows.shape[1], -1), 'ep', s...  5.94 us
    scatter x1, local copies, waits for them, and re-layouts, per_device(): send_block = jnp.zeros((peer_count * capacity, width), jnp.bfloat16).at[s...  3.36 us
    dot_general x1, matrix products, feed_forward(): jnp.dot(hidden, lower, preferred_element_type=jnp.float32)  2.57 us
  transfers between devices with their start and end apart: 1, of which 1 were waited for; matrix products, arithmetic and copies ran while one was open for 0% of the time, Pallas kernels for 0%

commit v1 on v0

--- a/solution.py
+++ b/solution.py
@@ -2,6 +2,39 @@
 import jax.numpy as jnp
 from jax import lax
 from jax.sharding import PartitionSpec as P
+from jax.lax import axis_index, axis_size, ppermute
+
+
+def _assign_frame(packet, array_axis):
+    packet = jnp.moveaxis(packet, 0, array_axis)
+    piece_out = packet.shape
+    local_next = packet.reshape(
+        *piece_out[:array_axis],
+        piece_out[array_axis] * piece_out[array_axis + 1],
+        *piece_out[array_axis + 2 :]
+    )
+    return local_next
+
+
+def pair_joints_up(work_x, device_axis, dim_no):
+    dev_n = axis_size(device_axis)
+    pages = list(map(lambda src_i: (src_i, (src_i + 1) % dev_n), range(dev_n)))
+    stack_in = [(jj, hop_no) for hop_no, jj in pages]
+    b_now, block_out = ([], [])
+    it = 0
+    while it < dev_n - 1:
+        if it % 2 == 0:
+            b_now.append(ppermute(b_now[-1] if b_now else work_x, device_axis, pages))
+        else:
+            last = ppermute(block_out[-1] if block_out else work_x, device_axis, stack_in)
+            block_out.append(last)
+        it += 1
+    local_part = jnp.stack([*b_now[::-1], work_x, *block_out])
+    everything = axis_index(device_axis)
+    x_next = everything - len(b_now)
+    local_part = local_part[(jnp.arange(dev_n) - x_next) % dev_n]
+    p_next = _assign_frame(local_part, dim_no)
+    return p_next
 
 
 def feed_forward(rows, pair, lower):
@@ -19,9 +52,7 @@
     gates = gate_fixed[0]
     route_table = jnp.concatenate([dest_ids[0], gates >> 8, gates & 255], axis=1)
     route_pad = jnp.pad(route_table, ((0, 0), (0, 128 - 3 * top_count))).astype(jnp.bfloat16)
-    packed = lax.all_gather(
-        jnp.concatenate([own_rows, route_pad], axis=1), "dp", axis=0, tiled=True
-    )
+    packed = pair_joints_up(jnp.concatenate([own_rows, route_pad], axis=1), "dp", 0)
     column_rows = packed[:, :width]
     table = packed[:, width : width + 3 * top_count].astype(jnp.int32)
     column_table = jnp.concatenate(

time: 123 us -> 124 us (level)
  blocking collectives: 69.9 us -> 56.6 us
  starting transfers between devices: 5.94 us -> 15.2 us
  waiting for transfers between devices: 31.2 us -> 35.8 us
    all_gather x1 -> x0, blocking collectives: 12.2 us -> none  [per_device(): lax.all_gather(jnp.concatenate([own_rows, route_pad], axis=1), 'dp', axis...]
    ppermute x0 -> x3, starting transfers between devices: none -> 9.24 us  [the longest x2 5.59 us: pair_joints_up(): b_now.append(ppermute(b_now[-1] if b_now else work_x, device_axis, pages))]
    ppermute x0 -> x3, waiting for transfers between devices: none -> 4.64 us  [the longest x2 4.64 us: pair_joints_up(): b_now.append(ppermute(b_now[-1] if b_now else work_x, device_axis, pages))]
  transfers between devices with their start and end apart: 1 -> 4, of which waited for: 1 -> 2; matrix products, arithmetic and copies ran while one was open for 0% -> 0% of each run, Pallas kernels for 0% -> 0%
where the time goes in v1:
time: 124 us
  blocking collectives  56.6 us (46%)
  waiting for transfers between devices  35.8 us (29%)
  starting transfers between devices  15.2 us (12%)
  local copies, waits for them, and re-layouts  8.22 us (7%)
  matrix products  4.21 us (3%)
  other arithmetic  3.49 us (3%)
    all_to_all x1, blocking collectives, per_device(): lax.all_to_all(send_block, 'ep', split_axis=0, concat_axis=0, tiled=True)  48.6 us
    all_to_all x1, waiting for transfers between devices, per_device(): lax.all_to_all(own_out.reshape(rows.shape[0], rows.shape[1], -1), 'ep', s...  31.2 us
    all_to_all x1, blocking collectives, per_device(): lax.all_to_all(summed.astype(jnp.bfloat16).reshape(4, -1, width), 'dp', s...  7.99 us
    all_to_all x1, starting transfers between devices, per_device(): lax.all_to_all(own_out.reshape(rows.shape[0], rows.shape[1], -1), 'ep', s...  5.93 us
    ppermute x2, starting transfers between devices, pair_joints_up(): b_now.append(ppermute(b_now[-1] if b_now else work_x, device_axis, pages))  5.59 us
    ppermute x2, waiting for transfers between devices, pair_joints_up(): b_now.append(ppermute(b_now[-1] if b_now else work_x, device_axis, pages))  4.64 us
    ppermute x1, starting transfers between devices, pair_joints_up(): ppermute(block_out[-1] if block_out else work_x, device_axis, stack_in)  3.65 us
    scatter x1, local copies, waits for them, and re-layouts, per_device(): send_block = jnp.zeros((peer_count * capacity, width), jnp.bfloat16).at[s...  3.36 us
  transfers between devices with their start and end apart: 4, of which 2 were waited for; matrix products, arithmetic and copies ran while one was open for 0% of the time, Pallas kernels for 0%

profile of v1, /device:TPU:8, one launch (start us, length us, event | category | flops | bytes accessed | tf_op | source)
XLA Modules:
  0.0 123.7 jit_solution(13121722479312869379)
XLA Ops:
  0.0 0.8 fusion.25
  0.8 0.1 fusion.28
  0.9 0.7 fusion.34
  1.6 3.4 %collective-permute-start = (bf16[4,2176]{1,0:T(4,128)(2,1)S(1)}, bf16[4,2176]{1,0:T(4,128)(2,1)S(1)}, u32[]{:S(2)}, u32[]{:S(2)}) collective-permute-start(bf16[4,2176]{1,0:T(4,128)(2,1)S(1)} %get-tuple-element.6), channel_id=1, source_target_pairs={{0,128},{128,256},{256,384},{384,0},{1,129},{129,257},{257,385},{3... | collective-permute-start | bytes 52232 | tf_op jit(solution)/shard_map/ppermute | solution.py:27
  5.0 3.7 %collective-permute-start.2 = (bf16[4,2176]{1,0:T(4,128)(2,1)S(1)}, bf16[4,2176]{1,0:T(4,128)(2,1)S(1)}, u32[]{:S(2)}, u32[]{:S(2)}) collective-permute-start(bf16[4,2176]{1,0:T(4,128)(2,1)S(1)} %get-tuple-element.6), channel_id=1, source_target_pairs={{128,0},{256,128},{384,256},{0,384},{129,1},{257,129},{385,257},{1... | collective-permute-start | bytes 52232 | tf_op jit(solution)/shard_map/ppermute | solution.py:29
  8.7 0.0 collective-permute-done
  8.7 2.2 %collective-permute-start.1 = (bf16[4,2176]{1,0:T(4,128)(2,1)S(1)}, bf16[4,2176]{1,0:T(4,128)(2,1)S(1)}, u32[]{:S(2)}, u32[]{:S(2)}) collective-permute-start(bf16[4,2176]{1,0:T(4,128)(2,1)S(1)} %collective-permute-done), channel_id=1, source_target_pairs={{0,128},{128,256},{256,384},{384,0},{1,129},{129,257},{257,385},{3... | collective-permute-start | bytes 52232 | tf_op jit(solution)/shard_map/ppermute | solution.py:27
  10.9 0.0 collective-permute-done.2
  10.9 4.6 %collective-permute-done.1 = bf16[4,2176]{1,0:T(4,128)(2,1)S(1)} collective-permute-done((bf16[4,2176]{1,0:T(4,128)(2,1)S(1)}, bf16[4,2176]{1,0:T(4,128)(2,1)S(1)}, u32[]{:S(2)}, u32[]{:S(2)}) %collective-permute-start.1) | collective-permute-done | bytes 17440 | tf_op jit(solution)/shard_map/ppermute | solution.py:27
  15.6 0.1 pad_maximum_fusion
  15.6 0.6 gather_fusion
  16.3 0.1 eq.17
  16.4 0.1 fusion.19
  16.5 0.2 reduce_window_sum.11
  16.7 0.2 select_reduce_fusion
  16.9 0.1 mul.43
  17.0 3.4 %scatter_custom_fusion = bf16[256,2048]{1,0:T(8,128)(2,1)S(1)} fusion(s32[128]{0:T(128)S(1)} %fusion.32, bf16[16,2048]{1,0:T(8,128)(2,1)S(1)} %slice.38, s32[1024]{0:T(1024)S(1)} %pad_clamp_fusion.1, bf16[]{:T(256)} %constant.53.clone.1), kind=kCustom, calls=%fused_computation.15 | custom fusion | bytes 1048578 | tf_op jit(solution)/shard_map/scatter | solution.py:79
  20.3 0.7 reshape.167
  21.0 48.6 %all_to_all.15 = bf16[128,2,2048]{2,1,0:T(2,128)(2,1)S(1)} all-to-all(bf16[128,2,2048]{2,1,0:T(2,128)(2,1)S(1)} %reshape.167), channel_id=1, replica_groups=mesh['dp'=4,'ep'=128] {'ep'}, dimensions={0} | all-to-all | bytes 2097152 | tf_op jit(solution)/shard_map/all_to_all | solution.py:82
  69.7 0.4 reshape.168
  70.1 1.6 %fusion.5 = f32[256,192]{0,1:T(8,128)S(1)} fusion(bf16[256,2048]{1,0:T(8,128)(2,1)S(1)} %reshape.168, bf16[1,2,192,2048]{3,2,1,0:T(8,128)(2,1)} %param.8), kind=kOutput, calls=%fused_computation.11 | convolution fusion | flops 201326592 | bytes 2031616 | tf_op jit(solution)/shard_map/nd,hd->nh/dot_general | solution.py:41
  71.7 2.6 %convolution_convert_fusion = bf16[256,2048]{1,0:T(8,128)(2,1)S(1)} fusion(bf16[256,2048]{1,0:T(8,128)(2,1)S(1)} %reshape.168, bf16[1,192,2048]{2,1,0:T(8,128)(2,1)S(1)} %copy-done, bf16[1,2,192,2048]{3,2,1,0:T(8,128)(2,1)} %param.8, f32[256,192]{0,1:T(8,128)S(1)} %fusion.5), kind=kOutput, calls=%fused_computation.4 | convolution fusion | flops 403472384 | bytes 3866624 | tf_op jit(solution)/shard_map/dot_general | solution.py:44
  74.3 1.5 %reshape.169 = bf16[128,2,2048]{2,1,0:T(2,128)(2,1)} reshape(bf16[256,2048]{1,0:T(8,128)(2,1)S(1)} %convolution_convert_fusion) | data formatting | bytes 2097152 | tf_op jit(solution)/shard_map/reshape | solution.py:86
  75.8 5.9 %all-to-all-start.1 = ((bf16[128,2,2048]{2,1,0:T(2,128)(2,1)}), bf16[128,2,2048]{2,1,0:T(2,128)(2,1)S(1)}, u32[]{:S(2)}, u32[]{:S(2)}) async-start(bf16[128,2,2048]{2,1,0:T(2,128)(2,1)} %reshape.169), calls=%async_computation.1 | async-start | bytes 2097152 | tf_op jit(solution)/shard_map/all_to_all | solution.py:85
  81.8 0.2 fusion.21
  82.0 0.1 broadcast_divide_fusion
  82.0 31.2 %all-to-all-done.1 = bf16[128,2,2048]{2,1,0:T(2,128)(2,1)S(1)} async-done(((bf16[128,2,2048]{2,1,0:T(2,128)(2,1)}), bf16[128,2,2048]{2,1,0:T(2,128)(2,1)S(1)}, u32[]{:S(2)}, u32[]{:S(2)}) %all-to-all-start.1) | async-done | bytes 1048608 | tf_op jit(solution)/shard_map/all_to_all | solution.py:85
  113.2 0.4 reshape.170
  113.6 0.9 gather_fusion.1
  114.6 0.5 fusion.1
  115.1 8.0 %all_to_all.16 = bf16[4,4,2048]{2,1,0:T(4,128)(2,1)S(1)} all-to-all(bf16[4,4,2048]{2,1,0:T(4,128)(2,1)S(1)} %convert_element_type.40), channel_id=1, replica_groups=mesh['dp'=4,'ep'=128] {'dp'}, dimensions={0} | all-to-all | bytes 131072 | tf_op jit(solution)/shard_map/all_to_all | solution.py:95
  123.1 0.6 reduce_sum.42
  (13 shorter events, 0.1 us)
Async XLA Ops:
  0.0 71.7 %copy-start = (bf16[1,192,2048]{2,1,0:T(8,128)(2,1)S(1)}, bf16[1,192,2048]{2,1,0:T(8,128)(2,1)}, u32[]{:S(2)}) copy-start(bf16[1,192,2048]{2,1,0:T(8,128)(2,1)} %param.9) | copy-start | bytes 2359300
  1.6 7.1 %collective-permute-start = (bf16[4,2176]{1,0:T(4,128)(2,1)S(1)}, bf16[4,2176]{1,0:T(4,128)(2,1)S(1)}, u32[]{:S(2)}, u32[]{:S(2)}) collective-permute-start(bf16[4,2176]{1,0:T(4,128)(2,1)S(1)} %get-tuple-element.6), channel_id=1, source_target_pairs={{0,128},{128,256},{256,384},{384,0},{1,129},{129,257},{257,385},{3... | collective-permute-start | bytes 52232 | tf_op jit(solution)/shard_map/ppermute | solution.py:27
  5.0 5.9 %collective-permute-start.2 = (bf16[4,2176]{1,0:T(4,128)(2,1)S(1)}, bf16[4,2176]{1,0:T(4,128)(2,1)S(1)}, u32[]{:S(2)}, u32[]{:S(2)}) collective-permute-start(bf16[4,2176]{1,0:T(4,128)(2,1)S(1)} %get-tuple-element.6), channel_id=1, source_target_pairs={{128,0},{256,128},{384,256},{0,384},{129,1},{257,129},{385,257},{1... | collective-permute-start | bytes 52232 | tf_op jit(solution)/shard_map/ppermute | solution.py:29
  8.7 6.9 %collective-permute-start.1 = (bf16[4,2176]{1,0:T(4,128)(2,1)S(1)}, bf16[4,2176]{1,0:T(4,128)(2,1)S(1)}, u32[]{:S(2)}, u32[]{:S(2)}) collective-permute-start(bf16[4,2176]{1,0:T(4,128)(2,1)S(1)} %collective-permute-done), channel_id=1, source_target_pairs={{0,128},{128,256},{256,384},{384,0},{1,129},{129,257},{257,385},{3... | collective-permute-start | bytes 52232 | tf_op jit(solution)/shard_map/ppermute | solution.py:27
  75.8 37.4 %all-to-all-start.1 = ((bf16[128,2,2048]{2,1,0:T(2,128)(2,1)}), bf16[128,2,2048]{2,1,0:T(2,128)(2,1)S(1)}, u32[]{:S(2)}, u32[]{:S(2)}) async-start(bf16[128,2,2048]{2,1,0:T(2,128)(2,1)} %reshape.169), calls=%async_computation.1 | async-start | bytes 2097152 | tf_op jit(solution)/shard_map/all_to_all | solution.py:85
